TPU v7x, 32 devices: a whole 2x2x4 slice. The times are simulated.
32 devices in a mesh: wide: 16 (over z, y, core), narrow: 2 (over x).
Axes of the slice: x: 2, y: 2, z: 4, core: 2. Of those that a mesh axis runs over, the one named last changes fastest.
Arguments:
- amplitudes: bfloat16 [65536, 1024], P(('wide', 'narrow')), may hold values from -0.046875 to 0.046875
- integral_slab: bfloat16 [65536, 1024], P(('wide', 'narrow')), may hold values from -0.046875 to 0.046875
- coupling: float32 [32, 1024, 1024], P(('wide', 'narrow')), may hold values from -0.046875 to 0.046875
- pair_of_block: int32 [32], replicated, may hold values from 0 to 31, each once
- pair_shift: float32 [32], replicated, may hold values from -4 to 4
- virt_energy: float32 [1024], replicated, may hold values from 0 to 26
- core_energy: float32 [64], replicated, may hold values from -6 to -4
- core_index: int32 [2], replicated, may hold values from 0 to 63, as said below
- frequency: float32 [16], replicated, may hold values from 6 to 30
- dipole: float32 [64, 1024], P(None, 'narrow'), may hold values from -6 to 6
Outputs:
- response: float32 [2, 32, 1024], P(None, None, 'narrow')
- residual_rms: float32 [2, 32], replicated
Inputs may be any that keep to these rules, and one draw needn't show every extreme that they name: `core_index`: the 2 core orbitals are different occupied orbitals, and the last of them is orbital 64 - 1.
All inputs are finite; a program needn't handle non-finite values.
Results may differ from a plain program's by a relative error of at most 0.0003.
Values sent between devices are 32-bit elements; how exact they have to be, the bound alone decides.
No kernel may reach another device: no remote copies, remote signals or barrier semaphores. Data moves between devices by JAX's collectives and lax.ppermute only.
A program may use at most 64 MiB of HBM per device.

v0:
```python
from functools import partial
import jax
import jax.numpy as jnp
from jax import lax
from jax.sharding import PartitionSpec as P

ITERS = 2
damping = 0.5
highest = lax.Precision.HIGHEST
contract_rows = (((0,), (0,)), ((), ()))
contract_last = (((1,), (1,)), ((), ()))
contract_pairs = (((0, 2), (0, 1)), ((), ()))


def divide_precond(real_part, imag_part, level, level_mag):
    return (
        (real_part * level - imag_part * damping) / level_mag,
        (imag_part * level + real_part * damping) / level_mag,
    )


def divide_denom(real_part, imag_part, denom_real, denom_mag):
    return (
        (real_part * denom_real + imag_part * damping) / denom_mag,
        (imag_part * denom_real - real_part * damping) / denom_mag,
    )


def apply_precond(real_part, imag_part, level):
    return (level * real_part + damping * imag_part, level * imag_part - damping * real_part)


def side_slab(slab_wide, total, flattened, start):
    return lax.dot_general(
        slab_wide, flattened, contract_last, precision=highest, preferred_element_type=jnp.float32
    )


def absorb(coupling, side, carry, piece, start):
    doubles_in, side_total = carry
    width = piece.shape[2]
    flattened = piece.reshape(-1, width)
    columns = coupling[0]
    updates = [
        lax.dot_general(
            flattened, columns, contract_last, precision=highest, preferred_element_type=jnp.float32
        )
    ]
    doubles_in = jnp.stack(updates, 0)
    side_total = side(side_total, flattened, start)
    return (doubles_in, side_total)


def per_device(
    amplitudes,
    integral_slab,
    coupling,
    pair_of_block,
    pair_shift,
    virt_energy,
    core_energy,
    core_index,
    frequency,
    dipole,
):
    virt_total = virt_energy.shape[0]
    block_rows = dipole.shape[1]
    row_start = lax.axis_index("narrow") * block_rows
    freq_count = frequency.shape[0]
    mode_count = freq_count * core_index.shape[0]
    local_pairs = coupling.shape[0]
    pair_count = pair_of_block.shape[0]
    local_rows = amplitudes.shape[0]
    chooser = (
        core_index[:, None] == jnp.arange(core_energy.shape[0], dtype=jnp.int32)[None, :]
    ).astype(jnp.float32)
    picked_energy = jnp.sum(chooser * core_energy[None, :], axis=1)
    picked_dipole = jnp.dot(chooser, dipole, precision=highest)
    shift = (frequency[None, :] + picked_energy[:, None]).reshape(-1)
    level = lax.dynamic_slice_in_dim(virt_energy, row_start, block_rows)[None, :] - shift[:, None]
    level_mag = level * level + damping * damping
    rhs = jnp.repeat(picked_dipole, freq_count, axis=0)
    slot_ids = lax.axis_index(("wide", "narrow")) * local_pairs + jnp.arange(
        local_pairs, dtype=jnp.int32
    )
    slot_match = slot_ids[:, None] == jnp.arange(pair_count, dtype=jnp.int32)[None, :]
    pair_ids = jnp.sum(jnp.where(slot_match, pair_of_block[None, :], 0), axis=1)
    pair_match = pair_ids[:, None] == jnp.arange(pair_count, dtype=jnp.int32)[None, :]
    slot_shift = jnp.sum(jnp.where(pair_match, pair_shift[None, :], 0.0), axis=1)
    denom_real = shift[None, :, None] - slot_shift[:, None, None] - virt_energy[None, None, :]
    denom_mag = denom_real * denom_real + damping * damping
    side = partial(side_slab, integral_slab.astype(jnp.float32))
    side_empty = jnp.zeros((local_rows, 2 * mode_count), jnp.float32)
    amplitudes_wide = amplitudes.astype(jnp.float32)
    resp_re, resp_im = divide_precond(rhs, jnp.zeros_like(rhs), level, level_mag)
    empty_doubles = jnp.zeros((local_pairs, 2 * mode_count, virt_total), jnp.float32)
    fold_plain = partial(absorb, coupling, side)
    rms_rows = []
    for sweep in range(ITERS):
        response = jnp.stack([resp_re, resp_im], 0)
        if sweep == 0:
            doubles_in, singles_term = fold_plain(
                (empty_doubles, side_empty),
                lax.all_gather(response, "narrow", axis=2, tiled=True),
                jnp.int32(0),
            )
        else:
            doubles_in, singles_term = fold_plain(
                (empty_doubles, side_empty),
                lax.all_gather(response, "narrow", axis=2, tiled=True),
                jnp.int32(0),
            )
        out_re, out_im = divide_denom(
            doubles_in[:, :mode_count], doubles_in[:, mode_count:], denom_real, denom_mag
        )
        outgoing = jnp.concatenate([out_re, out_im], 1)
        folded = lax.dot_general(
            outgoing,
            coupling,
            contract_pairs,
            precision=highest,
            preferred_element_type=jnp.float32,
        )
        folded = folded + lax.dot_general(
            singles_term,
            amplitudes_wide,
            contract_rows,
            precision=highest,
            preferred_element_type=jnp.float32,
        )
        summed = lax.psum(folded, ("wide", "narrow"))
        summed = lax.dynamic_slice_in_dim(summed, row_start, block_rows, 1)
        app_re, app_im = apply_precond(resp_re, resp_im, level)
        res_re = rhs - (app_re + summed[:mode_count])
        res_im = -(app_im + summed[mode_count:])
        partial_squares = jnp.sum(res_re * res_re + res_im * res_im, axis=1)
        total_squares = lax.psum(partial_squares, "narrow")
        rms_rows.append(jnp.sqrt(total_squares / (2 * virt_total) + 1e-06))
        step_re, step_im = divide_precond(res_re, res_im, level, level_mag)
        resp_re = resp_re + step_re
        resp_im = resp_im + step_im
    return (jnp.stack([resp_re, resp_im], 0), jnp.stack(rms_rows, 0))


def solution(mesh):
    placed = (
        P(("wide", "narrow"), None),
        P(("wide", "narrow"), None),
        P(("wide", "narrow"), None, None),
        P(),
        P(),
        P(),
        P(),
        P(),
        P(),
        P(None, "narrow"),
    )
    return jax.shard_map(
        per_device,
        mesh=mesh,
        in_specs=placed,
        out_specs=(P(None, None, "narrow"), P()),
        check_vma=False,
    )
```

profile of v0, /device:TPU:0, one launch (start us, length us, event | category | flops | bytes accessed | tf_op | source)
XLA Modules:
  0.0 329.7 jit_solution(13404999844428857127)
XLA Ops:
  7.2 0.0 copy-start
  7.2 0.0 all-reduce.4.cloned.1.call-start
  7.2 0.9 select_reduce_fusion
  8.1 0.7 broadcast_add_fusion
  8.8 0.1 add.152
  8.9 0.0 copy-done
  8.9 0.9 fusion.63
  9.8 0.0 copy-start.3
  9.8 1.4 fusion.64
  11.2 1.9 fusion.65
  13.1 0.6 broadcast_subtract_fusion
  13.8 0.8 dynamic_slice.9
  14.5 0.1 fusion.35
  14.7 7.1 %all_gather.6 = f32[2,32,1024]{2,1,0:T(8,128)S(1)} all-gather(f32[2,32,512]{2,1,0:T(8,128)S(1)} %pad_maximum_fusion), channel_id=1, replica_groups=mesh['wide'=16,'narrow'=2] {'narrow'}, dimensions={2}, use_global_device_ids=true | all-gather | bytes 393216 | tf_op jit(solution)/shard_map/all_gather | solution.py:104
  21.8 0.0 copy-start.7
  21.8 0.0 copy-start.5
  21.8 6.4 %fusion.8 = f32[1,64,1024]{2,1,0:T(8,128)S(1)} fusion(f32[64,1024]{1,0:T(8,128)S(1)} %bitcast.86, f32[1,1024,1024]{2,1,0:T(8,128)} %param.12), kind=kOutput, calls=%fused_computation.8 | convolution fusion | flops 805306368 | bytes 4718592 | tf_op jit(solution)/shard_map/dot_general | solution.py:45
  28.2 0.0 copy-done.3
  28.2 0.0 copy-start.1
  28.2 3.9 %fusion.71 = f32[64,2048]{1,0:T(8,128)S(1)} fusion(f32[64,1024]{1,0:T(8,128)S(1)} %bitcast.87, bf16[2048,1024]{1,0:T(8,128)(2,1)S(1)} %copy-done.3), kind=kOutput, calls=%fused_computation.100 | convolution fusion | flops 1610612736 | bytes 4980736 | tf_op jit(solution)/shard_map/dot_general | solution.py:34
  32.1 0.0 copy-done.7
  32.1 0.1 fusion.25
  32.2 0.0 copy-done.5
  32.3 2.3 fusion.72
  34.6 0.0 copy-done.1
  34.6 3.4 %fusion.11 = f32[64,1024]{1,0:T(8,128)} fusion(f32[64,1024]{1,0:T(8,128)S(1)} %fusion.72, f32[1,1024,1024]{2,1,0:T(8,128)S(1)} %copy-done.1, f32[1,32,1024]{2,1,0:T(8,128)S(1)} %get-tuple-element.13, f32[1,32,1024]{2,1,0:T(8,128)S(1)} %get-tuple-element.12), kind=kOutput, calls=%fused_computation.9 | convolution fusion | flops 805437440 | bytes 4980736 | tf_op jit(solution)/shard_map/dot_general | solution.py:117
  37.9 0.0 all-reduce.4.cloned.1.call-update
  38.0 0.0 all-reduce.6.cloned.1.call-start
  38.0 128.3 %all-reduce.4.cloned.1.call-done = f32[64,1024]{1,0:T(8,128)} async-done(((f32[64,1024]{1,0:T(8,128)}), f32[64,1024]{1,0:T(8,128)}) %all-reduce.4.cloned.1.call-update) | async-done | bytes 262160 | tf_op jit(solution)/shard_map/psum | solution.py:131
  166.3 0.0 copy-start.4
  166.3 1.2 add_reduce_fusion.1
  167.5 0.1 fusion.45
  167.7 5.8 %all_gather.7 = f32[2,32,1024]{2,1,0:T(8,128)S(1)} all-gather(f32[2,32,512]{2,1,0:T(8,128)S(1)} %pad_maximum_fusion.1), channel_id=1, replica_groups=mesh['wide'=16,'narrow'=2] {'narrow'}, dimensions={2}, use_global_device_ids=true | all-gather | bytes 393216 | tf_op jit(solution)/shard_map/all_gather | solution.py:110
  173.5 0.0 copy-start.6
  173.5 6.4 %fusion.14 = f32[1,64,1024]{2,1,0:T(8,128)S(1)} fusion(f32[64,1024]{1,0:T(8,128)S(1)} %bitcast.88, f32[1,1024,1024]{2,1,0:T(8,128)} %param.12), kind=kOutput, calls=%fused_computation.10 | convolution fusion | flops 805306368 | bytes 4718592 | tf_op jit(solution)/shard_map/dot_general | solution.py:45
  179.9 0.0 copy-done.4
  179.9 0.0 copy-start.2
  179.9 3.9 %fusion.73 = f32[64,2048]{1,0:T(8,128)S(1)} fusion(f32[64,1024]{1,0:T(8,128)S(1)} %bitcast.89, bf16[2048,1024]{1,0:T(8,128)(2,1)S(1)} %copy-done.4), kind=kOutput, calls=%fused_computation.102 | convolution fusion | flops 1610612736 | bytes 4980736 | tf_op jit(solution)/shard_map/dot_general | solution.py:34
  183.8 0.1 fusion.28
  183.9 0.0 copy-done.6
  183.9 2.3 fusion.74
  186.3 0.0 copy-done.2
  186.3 3.4 %fusion.17 = f32[64,1024]{1,0:T(8,128)} fusion(f32[64,1024]{1,0:T(8,128)S(1)} %fusion.74, f32[1,1024,1024]{2,1,0:T(8,128)S(1)} %copy-done.2, f32[1,32,1024]{2,1,0:T(8,128)S(1)} %get-tuple-element.11, f32[1,32,1024]{2,1,0:T(8,128)S(1)} %get-tuple-element.10), kind=kOutput, calls=%fused_computation.11 | convolution fusion | flops 805437440 | bytes 4980736 | tf_op jit(solution)/shard_map/dot_general | solution.py:117
  189.6 0.0 all-reduce.6.cloned.1.call-update
  189.6 125.8 %all-reduce.6.cloned.1.call-done = f32[64,1024]{1,0:T(8,128)} async-done(((f32[64,1024]{1,0:T(8,128)}), f32[64,1024]{1,0:T(8,128)}) %all-reduce.6.cloned.1.call-update) | async-done | bytes 262160 | tf_op jit(solution)/shard_map/psum | solution.py:131
  315.5 1.1 add_reduce_fusion
  316.5 0.1 fusion.48
  316.7 0.7 pad_maximum_fusion.2
  317.3 4.9 %all-reduce = (f32[32]{0:T(128)S(1)}, f32[32]{0:T(128)S(1)}) all-reduce(f32[32]{0:T(128)S(1)} %get-tuple-element.7, f32[32]{0:T(128)S(1)} %get-tuple-element.4), channel_id=1, replica_groups=mesh['wide'=16,'narrow'=2] {'narrow'}, use_global_device_ids=true, to_apply=%region_8.9 | all-reduce | flops 64 | bytes 512 | tf_op jit(solution)/shard_map/psum | solution.py:137
  322.2 0.6 pad_maximum_fusion.3
  (4 shorter events, 0.0 us)
Async XLA Ops:
  7.2 1.7 copy-start
  7.2 159.1 %all-reduce.4.cloned.1.call-start = ((), (), s32[]{:S(2)}) async-start(), calls=%async_computation | async-start | bytes 524288 | tf_op jit(solution)/shard_map/psum | solution.py:131
  9.8 18.4 %copy-start.3 = (bf16[2048,1024]{1,0:T(8,128)(2,1)S(1)}, bf16[2048,1024]{1,0:T(8,128)(2,1)}, u32[]{:S(2)}) copy-start(bf16[2048,1024]{1,0:T(8,128)(2,1)} %param.11) | copy-start | bytes 12582916
  21.8 10.3 %copy-start.7 = (f32[1024]{0:T(1024)S(1)}, f32[1024]{0:T(1024)}, u32[]{:S(2)}) copy-start(f32[1024]{0:T(1024)} %param.15) | copy-start | bytes 12292
  21.8 10.5 %copy-start.5 = (bf16[2048,1024]{1,0:T(8,128)(2,1)S(1)}, bf16[2048,1024]{1,0:T(8,128)(2,1)}, u32[]{:S(2)}) copy-start(bf16[2048,1024]{1,0:T(8,128)(2,1)} %param.10) | copy-start | bytes 12582916
  28.2 6.4 %copy-start.1 = (f32[1,1024,1024]{2,1,0:T(8,128)S(1)}, f32[1,1024,1024]{2,1,0:T(8,128)}, u32[]{:S(2)}) copy-start(f32[1,1024,1024]{2,1,0:T(8,128)} %param.12) | copy-start | bytes 12582916
  38.0 277.5 %all-reduce.6.cloned.1.call-start = ((), (), s32[]{:S(2)}) async-start(), calls=%async_computation.1 | async-start | bytes 524288 | tf_op jit(solution)/shard_map/psum | solution.py:131
  166.3 13.6 %copy-start.4 = (bf16[2048,1024]{1,0:T(8,128)(2,1)S(1)}, bf16[2048,1024]{1,0:T(8,128)(2,1)}, u32[]{:S(2)}) copy-start(bf16[2048,1024]{1,0:T(8,128)(2,1)} %param.11) | copy-start | bytes 12582916
  173.5 10.5 %copy-start.6 = (bf16[2048,1024]{1,0:T(8,128)(2,1)S(1)}, bf16[2048,1024]{1,0:T(8,128)(2,1)}, u32[]{:S(2)}) copy-start(bf16[2048,1024]{1,0:T(8,128)(2,1)} %param.10) | copy-start | bytes 12582916
  179.9 6.4 %copy-start.2 = (f32[1,1024,1024]{2,1,0:T(8,128)S(1)}, f32[1,1024,1024]{2,1,0:T(8,128)}, u32[]{:S(2)}) copy-start(f32[1,1024,1024]{2,1,0:T(8,128)} %param.12) | copy-start | bytes 12582916
Sparse Core Ops, SparseCore 0:
  38.1 128.1 all-reduce.3
  189.8 125.6 all-reduce.5
where the time goes:
time: 330 us
  waiting for transfers between devices  254 us (77%)
  matrix products  32.8 us (10%)
  blocking collectives  17.8 us (5%)
  between operations  14.2 us (4%)
  other arithmetic  9.76 us (3%)
    psum x2, waiting for transfers between devices, per_device(): summed = lax.psum(folded, ('wide', 'narrow'))  254 us
    all_gather x2, blocking collectives, per_device(): lax.all_gather(response, 'narrow', axis=2, tiled=True)  12.9 us
    dot_general x2, matrix products, absorb(): lax.dot_general(flattened, columns, contract_last, precision=highest, pre...  12.8 us
    dot_general x2, matrix products, side_slab(): lax.dot_general(slab_wide, flattened, contract_last, precision=highest, p...  7.81 us
    dot_general x2, matrix products, per_device(): lax.dot_general(outgoing, coupling, contract_pairs, precision=highest, pr...  6.71 us
  transfers between devices with their start and end apart: 2, of which 2 were waited for; matrix products, arithmetic and copies ran while one was open for 0% of the time, Pallas kernels for 0%

commit v1 on v0

--- a/solution.py
+++ b/solution.py
@@ -128,7 +128,7 @@
             precision=highest,
             preferred_element_type=jnp.float32,
         )
-        summed = lax.psum(folded, ("wide", "narrow"))
+        summed = jnp.sum(lax.all_gather(folded, ("wide", "narrow")), axis=0)
         summed = lax.dynamic_slice_in_dim(summed, row_start, block_rows, 1)
         app_re, app_im = apply_precond(resp_re, resp_im, level)
         res_re = rhs - (app_re + summed[:mode_count])

time: 330 us -> 237 us (0.72)
  waiting for transfers between devices: 254 us -> 155 us
  other arithmetic: 9.76 us -> 15.8 us
    psum x2 -> x0, waiting for transfers between devices: 254 us -> none  [per_device(): summed = lax.psum(folded, ('wide', 'narrow'))]
    all_gather x0 -> x2, waiting for transfers between devices: none -> 155 us  [per_device(): summed = jnp.sum(lax.all_gather(folded, ('wide', 'narrow')), axis=0)]
    reduce_sum x0 -> x2, other arithmetic: none -> 7.96 us  [per_device(): summed = jnp.sum(lax.all_gather(folded, ('wide', 'narrow')), axis=0)]
where the time goes in v1:
time: 237 us
  waiting for transfers between devices  155 us (65%)
  matrix products  32.8 us (14%)
  blocking collectives  18.7 us (8%)
  other arithmetic  15.8 us (7%)
  between operations  14.2 us (6%)
    all_gather x2, waiting for transfers between devices, per_device(): summed = jnp.sum(lax.all_gather(folded, ('wide', 'narrow')), axis=0)  155 us
    all_gather x2, blocking collectives, per_device(): lax.all_gather(response, 'narrow', axis=2, tiled=True)  13.7 us
    dot_general x2, matrix products, absorb(): lax.dot_general(flattened, columns, contract_last, precision=highest, pre...  12.8 us
    reduce_sum x2, other arithmetic, per_device(): summed = jnp.sum(lax.all_gather(folded, ('wide', 'narrow')), axis=0)  7.96 us
    dot_general x2, matrix products, side_slab(): lax.dot_general(slab_wide, flattened, contract_last, precision=highest, p...  7.8 us
    dot_general x2, matrix products, per_device(): lax.dot_general(outgoing, coupling, contract_pairs, precision=highest, pr...  6.74 us
    psum x1, blocking collectives, per_device(): total_squares = lax.psum(partial_squares, 'narrow')  4.91 us
  transfers between devices with their start and end apart: 2, of which 2 were waited for; matrix products, arithmetic and copies ran while one was open for 0% of the time, Pallas kernels for 0%

profile of v1, /device:TPU:0, one launch (start us, length us, event | category | flops | bytes accessed | tf_op | source)
XLA Modules:
  0.0 237.1 jit_solution(11385735491987669836)
XLA Ops:
  7.2 0.0 copy-start
  7.2 0.0 all-gather.5.cloned.1.call-start
  7.2 0.9 select_reduce_fusion
  8.1 0.7 broadcast_add_fusion
  8.8 0.1 add.148
  8.9 0.0 copy-done
  8.9 0.9 fusion.63
  9.8 0.0 copy-start.3
  9.8 1.4 fusion.64
  11.2 1.9 fusion.65
  13.1 0.6 broadcast_subtract_fusion
  13.8 0.8 dynamic_slice.9
  14.5 0.1 fusion.35
  14.7 7.1 %all_gather.18 = f32[2,32,1024]{2,1,0:T(8,128)S(1)} all-gather(f32[2,32,512]{2,1,0:T(8,128)S(1)} %pad_maximum_fusion), channel_id=1, replica_groups=mesh['wide'=16,'narrow'=2] {'narrow'}, dimensions={2}, use_global_device_ids=true | all-gather | bytes 393216 | tf_op jit(solution)/shard_map/all_gather | solution.py:104
  21.8 0.0 copy-start.7
  21.8 0.0 copy-start.5
  21.8 6.4 %fusion.8 = f32[1,64,1024]{2,1,0:T(8,128)S(1)} fusion(f32[64,1024]{1,0:T(8,128)S(1)} %bitcast.90, f32[1,1024,1024]{2,1,0:T(8,128)} %param.12), kind=kOutput, calls=%fused_computation.8 | convolution fusion | flops 805306368 | bytes 4718592 | tf_op jit(solution)/shard_map/dot_general | solution.py:45
  28.2 0.0 copy-done.3
  28.2 0.0 copy-start.1
  28.2 3.9 %fusion.71 = f32[64,2048]{1,0:T(8,128)S(1)} fusion(f32[64,1024]{1,0:T(8,128)S(1)} %bitcast.91, bf16[2048,1024]{1,0:T(8,128)(2,1)S(1)} %copy-done.3), kind=kOutput, calls=%fused_computation.100 | convolution fusion | flops 1610612736 | bytes 4980736 | tf_op jit(solution)/shard_map/dot_general | solution.py:34
  32.1 0.0 copy-done.7
  32.1 0.1 fusion.25
  32.2 0.0 copy-done.5
  32.2 2.3 fusion.72
  34.6 0.0 copy-done.1
  34.6 3.4 %fusion.11 = f32[64,1024]{1,0:T(8,128)} fusion(f32[64,1024]{1,0:T(8,128)S(1)} %fusion.72, f32[1,1024,1024]{2,1,0:T(8,128)S(1)} %copy-done.1, f32[1,32,1024]{2,1,0:T(8,128)S(1)} %get-tuple-element.13, f32[1,32,1024]{2,1,0:T(8,128)S(1)} %get-tuple-element.12), kind=kOutput, calls=%fused_computation.9 | convolution fusion | flops 805437440 | bytes 4980736 | tf_op jit(solution)/shard_map/dot_general | solution.py:117
  37.9 0.0 all-gather.5.cloned.1.call-update
  38.0 0.0 all-gather.7.cloned.1.call-start
  38.0 78.7 %all-gather.5.cloned.1.call-done = f32[2048,1024]{1,0:T(8,128)} async-done(((f32[64,1024]{1,0:T(8,128)}), f32[2048,1024]{1,0:T(8,128)}) %all-gather.5.cloned.1.call-update) | async-done | bytes 8388624 | tf_op jit(solution)/shard_map/all_gather | solution.py:131
  116.7 4.0 %reduce_sum.66 = f32[64,1024]{1,0:T(8,128)S(1)} reduce(f32[32,64,1024]{2,1,0:T(8,128)} %bitcast.88, f32[]{:T(128)} %constant.6.clone.1), dimensions={0}, to_apply=%region_3.4 | reduce | flops 2031616 | bytes 8650756 | tf_op jit(solution)/shard_map/reduce_sum | solution.py:131
  120.7 0.0 copy-start.4
  120.7 0.2 add_reduce_fusion.1
  120.9 0.1 fusion.45
  121.1 6.6 %all_gather.21 = f32[2,32,1024]{2,1,0:T(8,128)S(1)} all-gather(f32[2,32,512]{2,1,0:T(8,128)S(1)} %pad_maximum_fusion.1), channel_id=1, replica_groups=mesh['wide'=16,'narrow'=2] {'narrow'}, dimensions={2}, use_global_device_ids=true | all-gather | bytes 393216 | tf_op jit(solution)/shard_map/all_gather | solution.py:110
  127.7 0.0 copy-start.6
  127.7 6.4 %fusion.14 = f32[1,64,1024]{2,1,0:T(8,128)S(1)} fusion(f32[64,1024]{1,0:T(8,128)S(1)} %bitcast.92, f32[1,1024,1024]{2,1,0:T(8,128)} %param.12), kind=kOutput, calls=%fused_computation.10 | convolution fusion | flops 805306368 | bytes 4718592 | tf_op jit(solution)/shard_map/dot_general | solution.py:45
  134.1 0.0 copy-done.4
  134.1 0.0 copy-start.2
  134.1 3.9 %fusion.73 = f32[64,2048]{1,0:T(8,128)S(1)} fusion(f32[64,1024]{1,0:T(8,128)S(1)} %bitcast.93, bf16[2048,1024]{1,0:T(8,128)(2,1)S(1)} %copy-done.4), kind=kOutput, calls=%fused_computation.102 | convolution fusion | flops 1610612736 | bytes 4980736 | tf_op jit(solution)/shard_map/dot_general | solution.py:34
  138.0 0.1 fusion.28
  138.2 0.0 copy-done.6
  138.2 2.3 fusion.74
  140.5 0.0 copy-done.2
  140.5 3.4 %fusion.17 = f32[64,1024]{1,0:T(8,128)} fusion(f32[64,1024]{1,0:T(8,128)S(1)} %fusion.74, f32[1,1024,1024]{2,1,0:T(8,128)S(1)} %copy-done.2, f32[1,32,1024]{2,1,0:T(8,128)S(1)} %get-tuple-element.11, f32[1,32,1024]{2,1,0:T(8,128)S(1)} %get-tuple-element.10), kind=kOutput, calls=%fused_computation.11 | convolution fusion | flops 805437440 | bytes 4980736 | tf_op jit(solution)/shard_map/dot_general | solution.py:117
  143.9 0.0 all-gather.7.cloned.1.call-update
  143.9 75.9 %all-gather.7.cloned.1.call-done = f32[2048,1024]{1,0:T(8,128)} async-done(((f32[64,1024]{1,0:T(8,128)}), f32[2048,1024]{1,0:T(8,128)}) %all-gather.7.cloned.1.call-update) | async-done | bytes 8388624 | tf_op jit(solution)/shard_map/all_gather | solution.py:131
  219.8 4.0 %reduce_sum.67 = f32[64,1024]{1,0:T(8,128)S(1)} reduce(f32[32,64,1024]{2,1,0:T(8,128)} %bitcast.89, f32[]{:T(128)} %constant.6.clone.1), dimensions={0}, to_apply=%region_4.5 | reduce | flops 2031616 | bytes 8650756 | tf_op jit(solution)/shard_map/reduce_sum | solution.py:131
  223.8 0.2 add_reduce_fusion
  224.0 0.1 fusion.48
  224.1 0.7 pad_maximum_fusion.2
  224.8 4.9 %all-reduce = (f32[32]{0:T(128)S(1)}, f32[32]{0:T(128)S(1)}) all-reduce(f32[32]{0:T(128)S(1)} %get-tuple-element.7, f32[32]{0:T(128)S(1)} %get-tuple-element.4), channel_id=1, replica_groups=mesh['wide'=16,'narrow'=2] {'narrow'}, use_global_device_ids=true, to_apply=%region_8.9 | all-reduce | flops 64 | bytes 512 | tf_op jit(solution)/shard_map/psum | solution.py:137
  229.7 0.6 pad_maximum_fusion.3
  (4 shorter events, 0.0 us)
Async XLA Ops:
  7.2 1.7 copy-start
  7.2 109.5 %all-gather.5.cloned.1.call-start = ((), (), s32[]{:S(2)}) async-start(), calls=%async_computation | async-start | bytes 8650752 | tf_op jit(solution)/shard_map/all_gather | solution.py:131
  9.8 18.4 %copy-start.3 = (bf16[2048,1024]{1,0:T(8,128)(2,1)S(1)}, bf16[2048,1024]{1,0:T(8,128)(2,1)}, u32[]{:S(2)}) copy-start(bf16[2048,1024]{1,0:T(8,128)(2,1)} %param.11) | copy-start | bytes 12582916
  21.8 10.3 %copy-start.7 = (f32[1024]{0:T(1024)S(1)}, f32[1024]{0:T(1024)}, u32[]{:S(2)}) copy-start(f32[1024]{0:T(1024)} %param.15) | copy-start | bytes 12292
  21.8 10.5 %copy-start.5 = (bf16[2048,1024]{1,0:T(8,128)(2,1)S(1)}, bf16[2048,1024]{1,0:T(8,128)(2,1)}, u32[]{:S(2)}) copy-start(bf16[2048,1024]{1,0:T(8,128)(2,1)} %param.10) | copy-start | bytes 12582916
  28.2 6.4 %copy-start.1 = (f32[1,1024,1024]{2,1,0:T(8,128)S(1)}, f32[1,1024,1024]{2,1,0:T(8,128)}, u32[]{:S(2)}) copy-start(f32[1,1024,1024]{2,1,0:T(8,128)} %param.12) | copy-start | bytes 12582916
  38.0 181.8 %all-gather.7.cloned.1.call-start = ((), (), s32[]{:S(2)}) async-start(), calls=%async_computation.1 | async-start | bytes 8650752 | tf_op jit(solution)/shard_map/all_gather | solution.py:131
  120.7 13.4 %copy-start.4 = (bf16[2048,1024]{1,0:T(8,128)(2,1)S(1)}, bf16[2048,1024]{1,0:T(8,128)(2,1)}, u32[]{:S(2)}) copy-start(bf16[2048,1024]{1,0:T(8,128)(2,1)} %param.11) | copy-start | bytes 12582916
  127.7 10.5 %copy-start.6 = (bf16[2048,1024]{1,0:T(8,128)(2,1)S(1)}, bf16[2048,1024]{1,0:T(8,128)(2,1)}, u32[]{:S(2)}) copy-start(bf16[2048,1024]{1,0:T(8,128)(2,1)} %param.10) | copy-start | bytes 12582916
  134.1 6.4 %copy-start.2 = (f32[1,1024,1024]{2,1,0:T(8,128)S(1)}, f32[1,1024,1024]{2,1,0:T(8,128)}, u32[]{:S(2)}) copy-start(f32[1,1024,1024]{2,1,0:T(8,128)} %param.12) | copy-start | bytes 12582916
Sparse Core Ops, SparseCore 0:
  38.1 78.5 all-gather.4
  144.0 75.7 all-gather.6
